TPU v7x, 512 devices: a whole 4x4x16 slice. The times are simulated.
512 devices in a mesh: dp: 16 (over z), fsdp: 32 (over x, y, core).
Axes of the slice: x: 4, y: 4, z: 16, core: 2. Of those that a mesh axis runs over, the one named last changes fastest.
Arguments:
- txt_tokens: bfloat16 [512, 8, 3072], P(('dp', 'fsdp')), may hold values from -6 to 6
- concept_table: bfloat16 [4096, 3072], P('dp'), may hold values from -6 to 6
- concept_ids: int32 [512], P(('dp', 'fsdp')), may hold values from 0 to 4095
- positions: int32 [512], P(('dp', 'fsdp')), may hold values from 0 to 7
- timesteps: int32 [512], P(('dp', 'fsdp')), may hold values from 0 to 63
- counts: int32 [4096], P('dp'), may hold values from 1 to 16
- mod_table: bfloat16 [64, 2, 3072], P(None, None, 'fsdp'), may hold values from -1.5 to 1.5
- kv_weight: bfloat16 [3072, 3072], P('fsdp'), may hold values from -0.109375 to 0.109375
- kv_bias: float32 [3072], replicated, may hold values from -3 to 3
- key_gain: float32 [128], replicated, may hold values from 0.5 to 1.5
- img_query: bfloat16 [512, 192, 1536], P(('dp', 'fsdp')), may hold values from -256 to 256
- img_key: bfloat16 [512, 192, 1536], P(('dp', 'fsdp')), may hold values from -6 to 6
- img_value: bfloat16 [512, 192, 1536], P(('dp', 'fsdp')), may hold values from -6 to 6
- out_grad: bfloat16 [512, 192, 1536], P(('dp', 'fsdp')), may hold values from -6 to 6
Outputs:
- table_grad: float32 [4096, 3072], P('dp', 'fsdp')
Inputs may be any that keep to these rules, and one draw needn't show every extreme that they name: `concept_ids`: concept of each sample, some concepts far more common than others.
All inputs are finite; a program needn't handle non-finite values.
Results may differ from a plain program's by a relative error of at most 0.0083.
Values may be sent and summed in bfloat16 or wider, within the bound.
A program may use at most 64 MiB of HBM per device.

v0:
```python
import jax
import jax.numpy as jnp
from jax import lax
from jax.sharding import PartitionSpec as P

EPSILON = 1e-06


def layer_norm(values):
    centre = jnp.mean(values, -1, keepdims=True)
    spread = jnp.mean((values - centre) ** 2, -1, keepdims=True)
    inverse = lax.rsqrt(spread + EPSILON)
    return ((values - centre) * inverse, inverse[..., 0])


def shards(
    txt_tokens,
    concept_table,
    concept_ids,
    positions,
    timesteps,
    counts,
    mod_table,
    kv_weight,
    kv_bias,
    key_gain,
    img_query,
    img_key,
    img_value,
    out_grad,
):
    highest = lax.Precision.HIGHEST
    fsdp_size = lax.axis_size("fsdp")
    column = lax.axis_index("fsdp")
    tok_len = txt_tokens.shape[1]
    model_width = txt_tokens.shape[2]
    slice_width = kv_weight.shape[0]
    kv_width = kv_weight.shape[1]
    head_width = kv_width // 2
    head_dim = key_gain.shape[0]
    head_count = head_width // head_dim
    img_len = img_query.shape[1]
    bucket_count = mod_table.shape[0]
    root_dh = jnp.sqrt(jnp.float32(head_dim))
    table_hat, table_rstd = layer_norm(concept_table.astype(jnp.float32))
    table_part = lax.dynamic_slice_in_dim(
        table_hat.astype(jnp.bfloat16), column * slice_width, slice_width, 1
    )
    table_all = lax.all_gather(table_part, "dp", axis=0, tiled=True)
    own_hat = layer_norm(txt_tokens[0].astype(jnp.float32))[0].astype(jnp.bfloat16)
    labels = jnp.stack([concept_ids[0], positions[0], timesteps[0]])
    label_tile = jnp.tile(labels[None, :], (1, fsdp_size))
    token_cols, label_cols = (
        lax.all_to_all(own_hat, "fsdp", split_axis=1, concat_axis=0, tiled=True),
        lax.all_to_all(label_tile, "fsdp", split_axis=1, concat_axis=0, tiled=True),
    )
    group_ids = label_cols[:, 0]
    group_pos = label_cols[:, 1]
    group_time = label_cols[:, 2]
    concept_cols = jnp.take(table_all, group_ids, axis=0)
    token_cols = token_cols.reshape(fsdp_size, tok_len, slice_width)
    is_place = jnp.arange(tok_len, dtype=jnp.int32)[None, :] == group_pos[:, None]
    token_cols = jnp.where(is_place[:, :, None], concept_cols[:, None, :], token_cols)
    pick_time = (jnp.arange(bucket_count, dtype=jnp.int32)[None, :] == group_time[:, None]).astype(
        jnp.bfloat16
    )
    modulation = jnp.dot(
        pick_time,
        mod_table.reshape(bucket_count, 2 * slice_width),
        preferred_element_type=jnp.float32,
    )
    modulation = modulation.reshape(fsdp_size, 2, slice_width)
    shift_cols = modulation[:, 0]
    scale_cols = 1.0 + modulation[:, 1]
    modulated = (
        scale_cols[:, None, :] * token_cols.astype(jnp.float32) + shift_cols[:, None, :]
    ).astype(jnp.bfloat16)
    kv_terms = jnp.dot(
        modulated.reshape(fsdp_size * tok_len, slice_width),
        kv_weight,
        preferred_element_type=jnp.float32,
    )
    kv_terms = kv_terms.reshape(fsdp_size, tok_len, kv_width)
    weight_f = kv_weight.astype(jnp.float32)
    concept_f = concept_cols.astype(jnp.float32)
    side_rows = jnp.stack([scale_cols, scale_cols * concept_f], 1).reshape(
        fsdp_size * 2, slice_width
    )
    side_terms = jnp.dot(side_rows, weight_f, precision=highest).reshape(fsdp_size, 2, kv_width)
    all_terms = jnp.concatenate([kv_terms, side_terms], 1)
    row_block = all_terms.shape[1]
    all_terms = all_terms.reshape(fsdp_size * row_block, kv_width)
    own_rows = lax.psum_scatter(all_terms, "fsdp", scatter_dimension=0, tiled=True)
    kv_rows = own_rows[:tok_len] + kv_bias
    pos_pick = (jnp.arange(tok_len, dtype=jnp.int32) == positions[0]).astype(jnp.float32)
    key_raw = kv_rows[:, :head_width].reshape(tok_len, head_count, head_dim)
    key_inv = lax.rsqrt(jnp.mean(key_raw * key_raw, -1) + EPSILON)
    key_norm = (
        (key_raw * key_inv[..., None] * key_gain).astype(jnp.bfloat16).reshape(tok_len, head_width)
    )
    val_txt = kv_rows[:, head_width:].astype(jnp.bfloat16)
    keys_all = jnp.concatenate([key_norm, img_key[0]], 0).reshape(
        tok_len + img_len, head_count, head_dim
    )
    vals_all = jnp.concatenate([val_txt, img_value[0]], 0).reshape(
        tok_len + img_len, head_count, head_dim
    )
    queries = img_query[0].reshape(img_len, head_count, head_dim)
    scores = (
        jnp.einsum("qhd,khd->hqk", queries, keys_all, preferred_element_type=jnp.float32) / root_dh
    )
    row_top = jnp.max(scores, -1, keepdims=True)
    raised = jnp.exp(scores - row_top)
    prob_full = raised / jnp.sum(raised, -1, keepdims=True)
    prob_low = prob_full.astype(jnp.bfloat16)
    attended = jnp.einsum("hqk,khd->qhd", prob_low, vals_all, preferred_element_type=jnp.float32)
    grad_f = out_grad[0].reshape(img_len, head_count, head_dim).astype(jnp.float32)
    row_delta = jnp.einsum("qhd,qhd->hq", grad_f, attended)
    prob_pos = jnp.einsum("hqk,k->hq", prob_full[:, :, :tok_len], pos_pick, precision=highest)
    val_local = val_txt.reshape(tok_len, head_count, head_dim).astype(jnp.float32)
    val_pos = jnp.einsum("k,khd->hd", pos_pick, val_local, precision=highest)
    grad_prob = jnp.einsum("qhd,hd->hq", grad_f, val_pos, precision=highest)
    grad_score = prob_pos * (grad_prob - row_delta)
    grad_val = jnp.einsum("hq,qhd->hd", prob_pos, grad_f, precision=highest)
    grad_key = (
        jnp.einsum("hq,qhd->hd", grad_score, queries.astype(jnp.float32), precision=highest)
        / root_dh
    )
    raw_pos = jnp.einsum("k,khd->hd", pos_pick, key_raw, precision=highest)
    inv_pos = jnp.einsum("k,kh->h", pos_pick, key_inv, precision=highest)
    normed_key = raw_pos * inv_pos[:, None]
    grad_norm = grad_key * key_gain
    grad_raw = inv_pos[:, None] * (
        grad_norm - normed_key * jnp.mean(grad_norm * normed_key, -1, keepdims=True)
    )
    grad_kv = jnp.concatenate([grad_raw.reshape(head_width), grad_val.reshape(head_width)])[None, :]
    side_mean = (
        jnp.stack(
            [
                jnp.dot(grad_kv[0], own_rows[tok_len], precision=highest),
                jnp.dot(grad_kv[0], own_rows[tok_len + 1], precision=highest),
            ]
        )
        / model_width
    )
    grads_all, sides_all = (
        lax.all_gather(grad_kv, "fsdp", axis=0, tiled=True),
        lax.all_gather(side_mean[None, :], "fsdp", axis=0, tiled=True),
    )
    grad_cols = jnp.dot(grads_all, weight_f.T, precision=highest) * scale_cols
    row_grad = grad_cols - sides_all[:, 0:1] - concept_f * sides_all[:, 1:2]
    owner_scale = table_rstd / counts.astype(jnp.float32)
    conc_total = table_all.shape[0]
    one_hot = (jnp.arange(conc_total, dtype=jnp.int32)[:, None] == group_ids[None, :]).astype(
        jnp.float32
    )
    dense_rows = jnp.dot(one_hot, row_grad, precision=highest)
    owned_rows = lax.psum_scatter(dense_rows, "dp", scatter_dimension=0, tiled=True)
    return owned_rows * owner_scale[:, None]


def solution(mesh):
    placed = (
        P(("dp", "fsdp"), None, None),
        P("dp", None),
        P(("dp", "fsdp")),
        P(("dp", "fsdp")),
        P(("dp", "fsdp")),
        P("dp"),
        P(None, None, "fsdp"),
        P("fsdp", None),
        P(),
        P(),
        P(("dp", "fsdp"), None, None),
        P(("dp", "fsdp"), None, None),
        P(("dp", "fsdp"), None, None),
        P(("dp", "fsdp"), None, None),
    )
    return jax.shard_map(
        shards, mesh=mesh, in_specs=placed, out_specs=P("dp", "fsdp"), check_vma=False
    )
```

profile of v0, /device:TPU:2, one launch (start us, length us, event | category | flops | bytes accessed | tf_op | source)
XLA Modules:
  0.0 369.3 jit_solution(15416597220606547347)
XLA Ops:
  9.3 9.3 %all-to-all-start = ((s32[1,32,3]{2,0,1:T(1,128)}), s32[1,32,3]{2,0,1:T(1,128)S(1)}, u32[]{:S(2)}, u32[]{:S(2)}) async-start(s32[1,32,3]{2,0,1:T(1,128)} %tile.2), calls=%async_computation | async-start | bytes 32768 | tf_op jit(solution)/shard_map/all_to_all | solution.py:55
  18.6 0.9 convert_reduce_fusion.1
  19.6 0.9 reshape.234
  20.5 1.7 convert_reduce_fusion
  22.3 2.1 multiply_reduce_fusion
  25.0 1.1 fusion.32
  26.1 39.8 %all_gather.9 = bf16[4096,96]{1,0:T(8,128)(2,1)S(1)} all-gather(bf16[256,96]{1,0:T(8,128)(2,1)S(1)} %fusion.32), channel_id=1, replica_groups=mesh['dp'=16,'fsdp'=32] {'dp'}, dimensions={0}, use_global_device_ids=true | all-gather | bytes 835584 | tf_op jit(solution)/shard_map/all_gather | solution.py:49
  66.2 0.7 fusion.34
  67.1 7.4 %all-to-all-start.1 = ((bf16[8,32,96]{2,0,1:T(8,128)(2,1)}), bf16[8,32,96]{2,0,1:T(8,128)(2,1)S(1)}, u32[]{:S(2)}, u32[]{:S(2)}) async-start(bf16[8,32,96]{2,0,1:T(8,128)(2,1)} %fusion.34), calls=%async_computation.1 | async-start | bytes 131072 | tf_op jit(solution)/shard_map/all_to_all | solution.py:54
  77.8 3.0 all-to-all-done.1
  81.4 3.4 pad_maximum_fusion
  84.8 5.3 %reshape.229 = f32[320,3072]{1,0:T(8,128)} reshape(f32[32,10,3072]{2,1,0:T(8,128)} %pad_maximum_fusion) | data formatting | bytes 7864320 | tf_op jit(solution)/shard_map/reshape | solution.py:92
  90.2 1.0 copy-done.7
  92.8 2.2 reshape_squeeze.7
  95.0 1.3 dynamic-slice
  97.4 126.6 %all-reduce.3.cloned.1.call-done = f32[320,3072]{1,0:T(8,128)} async-done(((f32[320,3072]{1,0:T(8,128)}), f32[320,3072]{1,0:T(8,128)}) %all-reduce.3.cloned.1.call-update) | async-done | bytes 3932176
  224.0 0.9 dynamic-slice_add_fusion
  225.7 2.5 fusion.79
  229.1 0.6 copy-done.2
  229.8 0.9 multiply_reduce_fusion.1
  230.7 1.0 fusion.6
  231.9 2.1 fusion.26
  234.0 1.7 fusion.28
  236.9 1.0 constant_dynamic-slice_fusion.1
  237.9 0.7 multiply_reduce_fusion.3
  238.6 1.4 fusion.68
  240.0 20.8 %all-gather.1 = f32[32,1,2]{2,1,0:T(1,128)S(1)} all-gather(f32[1,1,2]{2,1,0:T(1,128)S(1)} %fusion.68), channel_id=1, replica_groups=mesh['dp'=16,'fsdp'=32] {'fsdp'}, dimensions={0}, use_global_device_ids=true | all-gather | bytes 264 | tf_op jit(solution)/shard_map/all_gather | solution.py:148
  260.9 24.3 %all-gather = f32[98304]{0:T(1024)S(1)} all-gather(f32[3072]{0:T(1024)S(1)} %get-tuple-element.7), channel_id=2, replica_groups=mesh['dp'=16,'fsdp'=32] {'fsdp'}, dimensions={0}, use_global_device_ids=true | all-gather | bytes 405504 | tf_op jit(solution)/shard_map/all_gather | solution.py:147
  285.2 0.7 fusion.11
  285.9 2.0 fusion.23
  287.9 73.0 %reduce-scatter.2.cloned.1.call-done = f32[256,96]{0,1:T(8,128)} async-done(((f32[4096,96]{0,1:T(8,128)}), f32[256,96]{0,1:T(8,128)}) %reduce-scatter.2.cloned.1.call-update) | async-done | bytes 98320 | tf_op jit(solution)/shard_map/reduce_scatter | solution.py:158
  360.9 1.5 broadcast_multiply_fusion
  (92 shorter events, 10.8 us)
Async XLA Ops:
  6.5 70.1 %copy-start = (bf16[96,3072]{1,0:T(8,128)(2,1)S(1)}, bf16[96,3072]{1,0:T(8,128)(2,1)}, u32[]{:S(2)}) copy-start(bf16[96,3072]{1,0:T(8,128)(2,1)} %param.21) | copy-start | bytes 1769476
  6.5 15.7 %copy-start.1 = (bf16[256,3072]{1,0:T(8,128)(2,1)S(1)}, bf16[256,3072]{1,0:T(8,128)(2,1)}, u32[]{:S(2)}) copy-start(bf16[256,3072]{1,0:T(8,128)(2,1)} %param.15) | copy-start | bytes 4718596
  9.3 57.8 %all-to-all-start = ((s32[1,32,3]{2,0,1:T(1,128)}), s32[1,32,3]{2,0,1:T(1,128)S(1)}, u32[]{:S(2)}, u32[]{:S(2)}) async-start(s32[1,32,3]{2,0,1:T(1,128)} %tile.2), calls=%async_computation | async-start | bytes 32768 | tf_op jit(solution)/shard_map/all_to_all | solution.py:55
  22.2 2.2 copy-start.18
  22.2 43.7 %copy-start.10 = (bf16[1,8,3072]{2,1,0:T(8,128)(2,1)S(1)}, bf16[1,8,3072]{2,1,0:T(8,128)(2,1)}, u32[]{:S(2)}) copy-start(bf16[1,8,3072]{2,1,0:T(8,128)(2,1)} %param.14) | copy-start | bytes 147460
  22.3 44.6 %copy-start.13 = (bf16[64,2,96]{2,1,0:T(2,128)(2,1)S(1)}, bf16[64,2,96]{2,1,0:T(2,128)(2,1)}, u32[]{:S(2)}) copy-start(bf16[64,2,96]{2,1,0:T(2,128)(2,1)} %param.20) | copy-start | bytes 73732
  67.1 13.7 %all-to-all-start.1 = ((bf16[8,32,96]{2,0,1:T(8,128)(2,1)}), bf16[8,32,96]{2,0,1:T(8,128)(2,1)S(1)}, u32[]{:S(2)}, u32[]{:S(2)}) async-start(bf16[8,32,96]{2,0,1:T(8,128)(2,1)} %fusion.34), calls=%async_computation.1 | async-start | bytes 131072 | tf_op jit(solution)/shard_map/all_to_all | solution.py:54
  74.5 149.5 %all-reduce.3.cloned.1.call-start = ((), (), s32[]{:S(2)}) async-start(), calls=%async_computation.4 | async-start | bytes 7864320
  76.0 0.6 copy-start.11
  90.1 1.1 copy-start.7
  90.1 1.5 copy-start.8
  90.1 2.1 copy-start.9
  90.1 270.8 %reduce-scatter.2.cloned.1.call-start = ((), (), s32[]{:S(2)}) async-start(), calls=%async_computation.3 | async-start | bytes 1671168 | tf_op jit(solution)/shard_map/reduce_scatter | solution.py:158
  91.6 133.6 %copy-start.4 = (bf16[192,12,128]{2,1,0:T(8,128)(2,1)}, bf16[192,12,128]{2,1,0:T(8,128)(2,1)S(1)}, u32[]{:S(2)}) copy-start(bf16[192,12,128]{2,1,0:T(8,128)(2,1)S(1)} %reshape_squeeze.6) | copy-start | bytes 1769476
  92.2 4.8 %copy-start.19 = (f32[128]{0:T(128)S(1)}, f32[128]{0:T(128)}, u32[]{:S(2)}) copy-start(f32[128]{0:T(128)} %param.23) | copy-start | bytes 1540
  92.6 131.4 %copy-start.14 = (f32[3072]{0:T(1024)S(1)}, f32[3072]{0:T(1024)}, u32[]{:S(2)}) copy-start(f32[3072]{0:T(1024)} %param.22) | copy-start | bytes 36868
  225.0 3.2 copy-start.5
  228.6 1.1 copy-start.2
  229.7 2.0 copy-start.6
  229.8 6.3 %copy-start.17 = (f32[128]{0:T(128)S(1)}, f32[128]{0:T(128)}, u32[]{:S(2)}) copy-start(f32[128]{0:T(128)} %broadcast_multiply_fusion.3) | copy-start | bytes 1540
  230.7 5.7 %copy-start.3 = (bf16[192,12,128]{2,1,0:T(8,128)(2,1)S(1)}, bf16[192,12,128]{2,1,0:T(8,128)(2,1)}, u32[]{:S(2)}) copy-start(bf16[192,12,128]{2,1,0:T(8,128)(2,1)} %reshape_squeeze.7) | copy-start | bytes 1769476
  230.7 54.6 %copy-start.12 = (f32[32,2,96]{2,0,1:T(8,128)S(1)}, f32[32,2,96]{2,0,1:T(8,128)}, u32[]{:S(2)}) copy-start(f32[32,2,96]{2,0,1:T(8,128)} %copy-done.11) | copy-start | bytes 73732
  231.7 54.2 %copy-start.16 = (s32[32]{0:T(128)S(1)}, s32[32]{0:T(128)}, u32[]{:S(2)}) copy-start(s32[32]{0:T(128)} %get-tuple-element.16) | copy-start | bytes 388
  285.2 75.7 %copy-start.15 = (f32[256]{0:T(256)S(1)}, f32[256]{0:T(256)}, u32[]{:S(2)}) copy-start(f32[256]{0:T(256)} %get-tuple-element.20) | copy-start | bytes 3076
Sparse Core Ops, SparseCore 0:
  90.2 133.7 all-reduce.2
  288.1 72.8 reduce-scatter.1
where the time goes:
time: 370 us; the launch traced here: 369 us
  waiting for transfers between devices  203 us (55%)
  blocking collectives  84.9 us (23%)
  other arithmetic  21 us (6%)
  starting transfers between devices  16.8 us (5%)
  local copies, waits for them, and re-layouts  16.7 us (5%)
  between operations  16.5 us (4%)
  matrix products  10.8 us (3%)
    unnamed x3, waiting for transfers between devices  127 us
    reduce_scatter x1, waiting for transfers between devices, shards(): lax.psum_scatter(dense_rows, 'dp', scatter_dimension=0, tiled=True)  73 us
    all_gather x1, blocking collectives, shards(): table_all = lax.all_gather(table_part, 'dp', axis=0, tiled=True)  39.8 us
    all_gather x1, blocking collectives, shards(): lax.all_gather(grad_kv, 'fsdp', axis=0, tiled=True)  24.3 us
    all_gather x1, blocking collectives, shards(): lax.all_gather(side_mean[None, :], 'fsdp', axis=0, tiled=True)  20.8 us
    all_to_all x1, starting transfers between devices, shards(): lax.all_to_all(label_tile, 'fsdp', split_axis=1, concat_axis=0, tiled=True)  9.32 us
  transfers between devices with their start and end apart: 4, of which 3 were waited for; matrix products, arithmetic and copies ran while one was open for 5% of the time, Pallas kernels for 0%

commit v1 on v0

--- a/solution.py
+++ b/solution.py
@@ -1,9 +1,20 @@
+import functools
 import jax
 import jax.numpy as jnp
 from jax import lax
 from jax.sharding import PartitionSpec as P
 
 EPSILON = 1e-06
+
+
+def rest_records(inputs, axis_key):
+    finding = jax.lax.axis_size(axis_key)
+    outer = jnp.stack([inputs] * finding)
+    value_now = jax.lax.all_to_all(outer, axis_key, 0, 0)
+    return jnp.concatenate(value_now, axis=0)
+
+
+advance_scenes = functools.partial(rest_records, axis_key="fsdp")
 
 
 def layer_norm(values):
@@ -144,7 +155,7 @@
         / model_width
     )
     grads_all, sides_all = (
-        lax.all_gather(grad_kv, "fsdp", axis=0, tiled=True),
+        advance_scenes(grad_kv),
         lax.all_gather(side_mean[None, :], "fsdp", axis=0, tiled=True),
     )
     grad_cols = jnp.dot(grads_all, weight_f.T, precision=highest) * scale_cols

time: 370 us -> 354 us (0.957)
  blocking collectives: 84.9 us -> 61.2 us
  starting transfers between devices: 16.8 us -> 23.6 us
    all_gather x1 -> x0, blocking collectives: 24.3 us -> none  [shards(): lax.all_gather(grad_kv, 'fsdp', axis=0, tiled=True)]
    all_to_all x0 -> x1, starting transfers between devices: none -> 6.62 us  [rest_records(): value_now = jax.lax.all_to_all(outer, axis_key, 0, 0)]
  transfers between devices with their start and end apart: 4 -> 5, of which waited for: 3 -> 3; matrix products, arithmetic and copies ran while one was open for 5% -> 5% of each run, Pallas kernels for 0% -> 0%
where the time goes in v1:
time: 354 us; the launch traced here: 353 us
  waiting for transfers between devices  202 us (57%)
  blocking collectives  61.2 us (17%)
  starting transfers between devices  23.6 us (7%)
  other arithmetic  20.9 us (6%)
  local copies, waits for them, and re-layouts  17.6 us (5%)
  between operations  16.5 us (5%)
  matrix products  10.7 us (3%)
    unnamed x3, waiting for transfers between devices  127 us
    reduce_scatter x1, waiting for transfers between devices, shards(): lax.psum_scatter(dense_rows, 'dp', scatter_dimension=0, tiled=True)  72.8 us
    all_gather x1, blocking collectives, shards(): table_all = lax.all_gather(table_part, 'dp', axis=0, tiled=True)  39.8 us
    all_gather x1, blocking collectives, shards(): lax.all_gather(side_mean[None, :], 'fsdp', axis=0, tiled=True)  21.3 us
    all_to_all x1, starting transfers between devices, shards(): lax.all_to_all(label_tile, 'fsdp', split_axis=1, concat_axis=0, tiled=True)  9.32 us
    all_to_all x1, starting transfers between devices, shards(): lax.all_to_all(own_hat, 'fsdp', split_axis=1, concat_axis=0, tiled=True)  7.39 us
  transfers between devices with their start and end apart: 5, of which 3 were waited for; matrix products, arithmetic and copies ran while one was open for 5% of the time, Pallas kernels for 0%

profile of v1, /device:TPU:2, one launch (start us, length us, event | category | flops | bytes accessed | tf_op | source)
XLA Modules:
  0.0 352.8 jit_solution(4657196009542717818)
XLA Ops:
  9.3 9.3 %all-to-all-start = ((s32[1,32,3]{2,0,1:T(1,128)}), s32[1,32,3]{2,0,1:T(1,128)S(1)}, u32[]{:S(2)}, u32[]{:S(2)}) async-start(s32[1,32,3]{2,0,1:T(1,128)} %tile.2), calls=%async_computation | async-start | bytes 32768 | tf_op jit(solution)/shard_map/all_to_all | solution.py:66
  18.6 0.9 convert_reduce_fusion.1
  19.6 0.9 reshape.240
  20.5 1.7 convert_reduce_fusion
  22.3 2.1 multiply_reduce_fusion
  25.0 1.1 fusion.34
  26.1 39.8 %all_gather.6 = bf16[4096,96]{1,0:T(8,128)(2,1)S(1)} all-gather(bf16[256,96]{1,0:T(8,128)(2,1)S(1)} %fusion.34), channel_id=1, replica_groups=mesh['dp'=16,'fsdp'=32] {'dp'}, dimensions={0}, use_global_device_ids=true | all-gather | bytes 835584 | tf_op jit(solution)/shard_map/all_gather | solution.py:60
  66.2 0.7 fusion.36
  67.1 7.4 %all-to-all-start.1 = ((bf16[8,32,96]{2,0,1:T(8,128)(2,1)}), bf16[8,32,96]{2,0,1:T(8,128)(2,1)S(1)}, u32[]{:S(2)}, u32[]{:S(2)}) async-start(bf16[8,32,96]{2,0,1:T(8,128)(2,1)} %fusion.36), calls=%async_computation.1 | async-start | bytes 131072 | tf_op jit(solution)/shard_map/all_to_all | solution.py:65
  78.0 2.9 all-to-all-done.1
  81.4 3.4 pad_maximum_fusion
  84.8 5.3 %reshape.234 = f32[320,3072]{1,0:T(8,128)} reshape(f32[32,10,3072]{2,1,0:T(8,128)} %pad_maximum_fusion) | data formatting | bytes 7864320 | tf_op jit(solution)/shard_map/reshape | solution.py:103
  90.1 1.0 copy-done.7
  92.8 2.2 reshape_squeeze.7
  95.0 1.3 dynamic-slice
  97.4 126.6 %all-reduce.3.cloned.1.call-done = f32[320,3072]{1,0:T(8,128)} async-done(((f32[320,3072]{1,0:T(8,128)}), f32[320,3072]{1,0:T(8,128)}) %all-reduce.3.cloned.1.call-update) | async-done | bytes 3932176
  224.0 0.9 dynamic-slice_add_fusion
  225.7 2.5 fusion.81
  229.1 0.6 copy-done.2
  229.8 0.9 multiply_reduce_fusion.1
  230.7 1.0 fusion.6
  231.9 2.1 fusion.26
  234.0 1.7 fusion.28
  236.9 1.0 constant_dynamic-slice_fusion.1
  237.9 0.7 multiply_reduce_fusion.3
  238.6 0.9 stack.22
  239.5 6.6 %all-to-all-start.2 = ((f32[32,1,3072]{2,1,0:T(1,128)}), f32[32,1,3072]{2,1,0:T(1,128)S(1)}, u32[]{:S(2)}, u32[]{:S(2)}) async-start(f32[32,1,3072]{2,1,0:T(1,128)} %stack.22), calls=%async_computation.2 | async-start | bytes 786432 | tf_op jit(solution)/shard_map/all_to_all | solution.py:13
  246.2 1.3 fusion.70
  247.6 21.3 %all-gather = f32[32,1,2]{2,1,0:T(1,128)S(1)} all-gather(f32[1,1,2]{2,1,0:T(1,128)S(1)} %fusion.70), channel_id=1, replica_groups=mesh['dp'=16,'fsdp'=32] {'fsdp'}, dimensions={0}, use_global_device_ids=true | all-gather | bytes 264 | tf_op jit(solution)/shard_map/all_gather | solution.py:159
  269.6 2.0 fusion.23
  271.6 72.8 %reduce-scatter.2.cloned.1.call-done = f32[256,96]{0,1:T(8,128)} async-done(((f32[4096,96]{0,1:T(8,128)}), f32[256,96]{0,1:T(8,128)}) %reduce-scatter.2.cloned.1.call-update) | async-done | bytes 98320 | tf_op jit(solution)/shard_map/reduce_scatter | solution.py:169
  344.4 1.5 broadcast_multiply_fusion
  (93 shorter events, 11.6 us)
Async XLA Ops:
  6.5 70.3 %copy-start = (bf16[96,3072]{1,0:T(8,128)(2,1)S(1)}, bf16[96,3072]{1,0:T(8,128)(2,1)}, u32[]{:S(2)}) copy-start(bf16[96,3072]{1,0:T(8,128)(2,1)} %param.21) | copy-start | bytes 1769476
  6.5 15.7 %copy-start.1 = (bf16[256,3072]{1,0:T(8,128)(2,1)S(1)}, bf16[256,3072]{1,0:T(8,128)(2,1)}, u32[]{:S(2)}) copy-start(bf16[256,3072]{1,0:T(8,128)(2,1)} %param.15) | copy-start | bytes 4718596
  9.3 57.8 %all-to-all-start = ((s32[1,32,3]{2,0,1:T(1,128)}), s32[1,32,3]{2,0,1:T(1,128)S(1)}, u32[]{:S(2)}, u32[]{:S(2)}) async-start(s32[1,32,3]{2,0,1:T(1,128)} %tile.2), calls=%async_computation | async-start | bytes 32768 | tf_op jit(solution)/shard_map/all_to_all | solution.py:66
  22.2 2.2 copy-start.18
  22.2 43.7 %copy-start.10 = (bf16[1,8,3072]{2,1,0:T(8,128)(2,1)S(1)}, bf16[1,8,3072]{2,1,0:T(8,128)(2,1)}, u32[]{:S(2)}) copy-start(bf16[1,8,3072]{2,1,0:T(8,128)(2,1)} %param.14) | copy-start | bytes 147460
  22.3 44.6 %copy-start.13 = (bf16[64,2,96]{2,1,0:T(2,128)(2,1)S(1)}, bf16[64,2,96]{2,1,0:T(2,128)(2,1)}, u32[]{:S(2)}) copy-start(bf16[64,2,96]{2,1,0:T(2,128)(2,1)} %param.20) | copy-start | bytes 73732
  67.1 13.7 %all-to-all-start.1 = ((bf16[8,32,96]{2,0,1:T(8,128)(2,1)}), bf16[8,32,96]{2,0,1:T(8,128)(2,1)S(1)}, u32[]{:S(2)}, u32[]{:S(2)}) async-start(bf16[8,32,96]{2,0,1:T(8,128)(2,1)} %fusion.36), calls=%async_computation.1 | async-start | bytes 131072 | tf_op jit(solution)/shard_map/all_to_all | solution.py:65
  74.5 149.5 %all-reduce.3.cloned.1.call-start = ((), (), s32[]{:S(2)}) async-start(), calls=%async_computation.5 | async-start | bytes 7864320
  76.2 0.6 copy-start.11
  90.1 1.1 copy-start.7
  90.1 1.5 copy-start.8
  90.1 2.1 copy-start.9
  91.6 133.6 %copy-start.4 = (bf16[192,12,128]{2,1,0:T(8,128)(2,1)}, bf16[192,12,128]{2,1,0:T(8,128)(2,1)S(1)}, u32[]{:S(2)}) copy-start(bf16[192,12,128]{2,1,0:T(8,128)(2,1)S(1)} %reshape_squeeze.6) | copy-start | bytes 1769476
  92.2 4.8 %copy-start.19 = (f32[128]{0:T(128)S(1)}, f32[128]{0:T(128)}, u32[]{:S(2)}) copy-start(f32[128]{0:T(128)} %param.23) | copy-start | bytes 1540
  92.6 131.4 %copy-start.14 = (f32[3072]{0:T(1024)S(1)}, f32[3072]{0:T(1024)}, u32[]{:S(2)}) copy-start(f32[3072]{0:T(1024)} %param.22) | copy-start | bytes 36868
  225.0 3.2 copy-start.5
  228.6 1.1 copy-start.2
  229.7 2.0 copy-start.6
  229.8 6.3 %copy-start.17 = (f32[128]{0:T(128)S(1)}, f32[128]{0:T(128)}, u32[]{:S(2)}) copy-start(f32[128]{0:T(128)} %broadcast_multiply_fusion.3) | copy-start | bytes 1540
  230.7 5.7 %copy-start.3 = (bf16[192,12,128]{2,1,0:T(8,128)(2,1)S(1)}, bf16[192,12,128]{2,1,0:T(8,128)(2,1)}, u32[]{:S(2)}) copy-start(bf16[192,12,128]{2,1,0:T(8,128)(2,1)} %reshape_squeeze.7) | copy-start | bytes 1769476
  230.7 38.3 %copy-start.12 = (f32[32,2,96]{2,0,1:T(8,128)S(1)}, f32[32,2,96]{2,0,1:T(8,128)}, u32[]{:S(2)}) copy-start(f32[32,2,96]{2,0,1:T(8,128)} %copy-done.11) | copy-start | bytes 73732
  231.7 37.9 %copy-start.16 = (s32[32]{0:T(128)S(1)}, s32[32]{0:T(128)}, u32[]{:S(2)}) copy-start(s32[32]{0:T(128)} %get-tuple-element.16) | copy-start | bytes 388
  239.5 104.9 %copy-start.15 = (f32[256]{0:T(256)S(1)}, f32[256]{0:T(256)}, u32[]{:S(2)}) copy-start(f32[256]{0:T(256)} %get-tuple-element.20) | copy-start | bytes 3076
  239.5 29.4 %all-to-all-start.2 = ((f32[32,1,3072]{2,1,0:T(1,128)}), f32[32,1,3072]{2,1,0:T(1,128)S(1)}, u32[]{:S(2)}, u32[]{:S(2)}) async-start(f32[32,1,3072]{2,1,0:T(1,128)} %stack.22), calls=%async_computation.2 | async-start | bytes 786432 | tf_op jit(solution)/shard_map/all_to_all | solution.py:13
  246.2 98.2 %reduce-scatter.2.cloned.1.call-start = ((), (), s32[]{:S(2)}) async-start(), calls=%async_computation.4 | async-start | bytes 1671168 | tf_op jit(solution)/shard_map/reduce_scatter | solution.py:169
Sparse Core Ops, SparseCore 0:
  90.2 133.7 all-reduce.2
  271.7 72.6 reduce-scatter.1
